TPU v7x, 128 devices: a whole 4x4x4 slice. The times are simulated.
128 devices in a mesh: walker: 16 (over x, y_hi, core), prow: 2 (over y_lo), pcol: 4 (over z).
Axes of the slice: x: 4, y: 4 (y_hi: 2, y_lo: 2; y = y_hi * 2 + y_lo), z: 4, core: 2. Of those that a mesh axis runs over, the one named last changes fastest.
Arguments:
- o_rows: bfloat16 [32768, 2048], P('walker', ('prow', 'pcol')), may hold values from -21 to 21
- o_cols: bfloat16 [32768, 4096], P('walker', ('pcol', 'prow')), may hold values from -48 to 48
- grad_energy: bfloat16 [32768, 4096], P('walker', ('pcol', 'prow')), may hold values from -8 to 8
- energy: float32 [32768], P('walker'), may hold values from -5 to 1
Outputs:
- hamil: float32 [2048, 4096], P(('prow', 'walker'), 'pcol')
- correlation: float32 [2048, 4096], P(('prow', 'walker'), 'pcol')
All inputs are finite; a program needn't handle non-finite values.
Results may differ from a plain program's by a relative error of at most 0.008.
Values may be sent and summed in bfloat16 or wider, within the bound.
A program may use at most 128 MiB of HBM per device.

v0:
```python
import jax
import jax.numpy as jnp
from jax import lax
from jax.sharding import PartitionSpec as P


def column_sums(values):
    return jnp.sum(values.astype(jnp.float32), axis=0)


def tile_product(row_tile, right_tile):
    return lax.dot_general(
        row_tile, right_tile, (((0,), (0,)), ((), ())), preferred_element_type=jnp.float32
    )


def per_device(o_rows, o_cols, grad_energy, energy):
    count = energy.shape[0] * lax.axis_size("walker")
    row_total, col_total = lax.psum((column_sums(o_rows), column_sums(o_cols)), "walker")
    row_shard = (o_rows - row_total / count).astype(jnp.bfloat16)
    col_shard = (o_cols - col_total / count).astype(jnp.bfloat16)
    row_tile = lax.all_gather(row_shard, "pcol", axis=1, tiled=True)
    col_tile, grad_tile = (
        lax.all_gather(col_shard, "prow", axis=1, tiled=True),
        lax.all_gather(grad_energy, "prow", axis=1, tiled=True),
    )
    weighted = (energy[:, None] * col_tile + grad_tile).astype(jnp.bfloat16)
    paired = jnp.concatenate((col_tile, weighted), axis=1)
    summed = lax.psum_scatter(
        tile_product(row_tile, paired), "walker", scatter_dimension=0, tiled=True
    )
    width = col_tile.shape[1]
    correlation = summed[:, :width]
    hamil = summed[:, width:]
    return (hamil / count, correlation / count)


def solution(mesh):
    in_specs = (
        P("walker", ("prow", "pcol")),
        P("walker", ("pcol", "prow")),
        P("walker", ("pcol", "prow")),
        P("walker"),
    )
    out_specs = (P(("prow", "walker"), "pcol"), P(("prow", "walker"), "pcol"))
    return jax.shard_map(
        per_device, mesh=mesh, in_specs=in_specs, out_specs=out_specs, check_vma=False
    )
```

profile of v0, /device:TPU:0, one launch (start us, length us, event | category | flops | bytes accessed | tf_op | source)
XLA Modules:
  0.0 314.8 jit_solution(17419922395982080322)
XLA Ops:
  7.2 0.0 copy-start
  7.2 0.0 all-gather.8.cloned.1.call-start
  7.2 0.7 all-gather.8.cloned.1.call-update
  7.9 0.0 all-gather.6.cloned.1.call-start
  8.0 1.5 convert_reduce_fusion.1
  9.5 0.0 copy-start.1
  9.5 0.3 convert_reduce_fusion
  9.8 38.7 %all-reduce = (f32[256]{0:T(256)S(1)}, f32[512]{0:T(512)S(1)}) all-reduce(f32[256]{0:T(256)S(1)} %convert_reduce_fusion.1, f32[512]{0:T(512)S(1)} %convert_reduce_fusion), channel_id=1, replica_groups=mesh['walker'=16,'prow'=2,'pcol'=4] {'walker'}, use_global_device_ids=true, to_apply=%region_1.0 | all-reduce | flops 768 | bytes 6144 | tf_op jit(solution)/shard_map/psum | solution.py:19
  48.5 1.8 fusion.4
  50.3 0.0 all-gather.6.cloned.1.call-update
  50.3 0.0 all-gather.4.cloned.1.call-start
  50.4 0.0 copy-done.1
  50.4 1.2 fusion.5
  51.6 0.0 all-gather.4.cloned.1.call-update
  51.6 0.0 reduce-scatter.2.cloned.1.call-start
  51.7 20.1 %all-gather.8.cloned.1.call-done = bf16[2048,1024]{1,0:T(8,128)(2,1)} async-done(((bf16[2048,512]{1,0:T(8,128)(2,1)}), bf16[2048,1024]{1,0:T(8,128)(2,1)}) %all-gather.8.cloned.1.call-update) | async-done | bytes 4194320 | tf_op jit(solution)/shard_map/all_gather | solution.py:25
  71.8 61.9 %all-gather.6.cloned.1.call-done = bf16[2048,1024]{1,0:T(8,128)(2,1)} async-done(((bf16[2048,512]{1,0:T(8,128)(2,1)}), bf16[2048,1024]{1,0:T(8,128)(2,1)}) %all-gather.6.cloned.1.call-update) | async-done | bytes 4194320 | tf_op jit(solution)/shard_map/all_gather | solution.py:24
  133.7 0.0 copy-done.2
  133.7 5.4 %add_convert_fusion = bf16[2048,1024]{1,0:T(8,128)(2,1)} fusion(bf16[2048,1024]{1,0:T(8,128)(2,1)} %all-gather.8.cloned.1.call-done, bf16[2048,1024]{1,0:T(8,128)(2,1)} %all-gather.6.cloned.1.call-done, f32[2048]{0:T(1024)S(1)} %copy-done.2), kind=kLoop, calls=%fused_computation.4 | loop fusion | flops 10485760 | bytes 12591104 | tf_op jit(solution)/shard_map/convert_element_type | solution.py:27
  139.1 48.8 %all-gather.4.cloned.1.call-done = bf16[2048,1024]{1,0:T(8,128)(2,1)} async-done(((bf16[2048,256]{1,0:T(8,128)(2,1)}), bf16[2048,1024]{1,0:T(8,128)(2,1)}) %all-gather.4.cloned.1.call-update) | async-done | bytes 4194320 | tf_op jit(solution)/shard_map/all_gather | solution.py:22
  187.9 15.2 %fusion = f32[1024,2048]{1,0:T(8,128)} fusion(bf16[2048,1024]{1,0:T(8,128)(2,1)} %all-gather.4.cloned.1.call-done, bf16[2048,1024]{1,0:T(8,128)(2,1)} %add_convert_fusion, bf16[2048,1024]{1,0:T(8,128)(2,1)} %all-gather.6.cloned.1.call-done), kind=kOutput, calls=%fused_computation | convolution fusion | flops 8606711808 | bytes 20971520 | tf_op jit(solution)/shard_map/dot_general | solution.py:12
  203.1 0.0 reduce-scatter.2.cloned.1.call-update
  203.1 103.3 %reduce-scatter.2.cloned.1.call-done = f32[64,2048]{1,0:T(8,128)} async-done(((f32[1024,2048]{1,0:T(8,128)}), f32[64,2048]{1,0:T(8,128)}) %reduce-scatter.2.cloned.1.call-update) | async-done | bytes 524304 | tf_op jit(solution)/shard_map/reduce_scatter | solution.py:29
  306.4 1.9 slice_multiply_fusion
  (4 shorter events, 0.0 us)
Async XLA Ops:
  7.2 2.3 copy-start
  7.2 64.6 %all-gather.8.cloned.1.call-start = ((), (), s32[]{:S(2)}) async-start(), calls=%async_computation.3 | async-start | bytes 6291456 | tf_op jit(solution)/shard_map/all_gather | solution.py:25
  7.9 125.8 %all-gather.6.cloned.1.call-start = ((), (), s32[]{:S(2)}) async-start(), calls=%async_computation.2 | async-start | bytes 6291456 | tf_op jit(solution)/shard_map/all_gather | solution.py:24
  9.5 40.9 %copy-start.1 = (bf16[2048,256]{1,0:T(8,128)(2,1)S(1)}, bf16[2048,256]{1,0:T(8,128)(2,1)}, u32[]{:S(2)}) copy-start(bf16[2048,256]{1,0:T(8,128)(2,1)} %param.4) | copy-start | bytes 3145732
  48.5 85.1 %copy-start.2 = (f32[2048]{0:T(1024)S(1)}, f32[2048]{0:T(1024)}, u32[]{:S(2)}) copy-start(f32[2048]{0:T(1024)} %param.7) | copy-start | bytes 24580
  50.3 137.6 %all-gather.4.cloned.1.call-start = ((), (), s32[]{:S(2)}) async-start(), calls=%async_computation.1 | async-start | bytes 5242880 | tf_op jit(solution)/shard_map/all_gather | solution.py:22
  51.6 254.8 %reduce-scatter.2.cloned.1.call-start = ((), (), s32[]{:S(2)}) async-start(), calls=%async_computation.4 | async-start | bytes 8912896 | tf_op jit(solution)/shard_map/reduce_scatter | solution.py:29
Sparse Core Ops, SparseCore 0:
  9.6 62.1 all-gather.7
  73.5 60.1 all-gather.5
  135.3 52.5 all-gather.3
  203.2 103.1 reduce-scatter.1
where the time goes:
time: 315 us
  waiting for transfers between devices  235 us (75%)
  blocking collectives  38.7 us (12%)
  matrix products  15.2 us (5%)
  between operations  13.8 us (4%)
  other arithmetic  12.2 us (4%)
    reduce_scatter x1, waiting for transfers between devices, per_device(): lax.psum_scatter(tile_product(row_tile, paired), 'walker', scatter_dimens...  103 us
    all_gather x1, waiting for transfers between devices, per_device(): lax.all_gather(col_shard, 'prow', axis=1, tiled=True)  61.9 us
    all_gather x1, waiting for transfers between devices, per_device(): row_tile = lax.all_gather(row_shard, 'pcol', axis=1, tiled=True)  48.8 us
    psum x1, blocking collectives, per_device(): lax.psum((column_sums(o_rows), column_sums(o_cols)), 'walker')  38.7 us
    all_gather x1, waiting for transfers between devices, per_device(): lax.all_gather(grad_energy, 'prow', axis=1, tiled=True)  20.1 us
    dot_general x1, matrix products, tile_product(): lax.dot_general(row_tile, right_tile, (((0,), (0,)), ((), ())), preferred...  15.2 us
  transfers between devices with their start and end apart: 4, of which 4 were waited for; matrix products, arithmetic and copies ran while one was open for 3% of the time, Pallas kernels for 0%

commit v1 on v0

--- a/solution.py
+++ b/solution.py
@@ -21,7 +21,9 @@
     col_shard = (o_cols - col_total / count).astype(jnp.bfloat16)
     row_tile = lax.all_gather(row_shard, "pcol", axis=1, tiled=True)
     col_tile, grad_tile = (
-        lax.all_gather(col_shard, "prow", axis=1, tiled=True),
+        jnp.concatenate(
+            lax.all_to_all(jnp.stack([col_shard] * lax.axis_size("prow")), "prow", 0, 0), axis=1
+        ),
         lax.all_gather(grad_energy, "prow", axis=1, tiled=True),
     )
     weighted = (energy[:, None] * col_tile + grad_tile).astype(jnp.bfloat16)

time: 315 us -> 278 us (0.88)
  waiting for transfers between devices: 235 us -> 130 us
  blocking collectives: 38.7 us -> 105 us
    all_to_all x0 -> x1, blocking collectives: none -> 65.9 us  [per_device(): lax.all_to_all(jnp.stack([col_shard] * lax.axis_size('prow')), 'prow', 0, 0)]
    all_gather x1 -> x0, waiting for transfers between devices: 61.9 us -> none  [per_device(): lax.all_gather(col_shard, 'prow', axis=1, tiled=True)]
    all_gather x1, waiting for transfers between devices: 48.8 us -> 26.3 us  [per_device(): row_tile = lax.all_gather(row_shard, 'pcol', axis=1, tiled=True)]
    all_gather x1, waiting for transfers between devices: 20.1 us -> 0.01 us  [per_device(): lax.all_gather(grad_energy, 'prow', axis=1, tiled=True)]
  transfers between devices with their start and end apart: 4 -> 3, of which waited for: 4 -> 2; matrix products, arithmetic and copies ran while one was open for 3% -> 4% of each run, Pallas kernels for 0% -> 0%
where the time goes in v1:
time: 278 us
  waiting for transfers between devices  130 us (47%)
  blocking collectives  105 us (38%)
  matrix products  15.2 us (5%)
  between operations  13.8 us (5%)
  other arithmetic  11.2 us (4%)
    reduce_scatter x1, waiting for transfers between devices, per_device(): lax.psum_scatter(tile_product(row_tile, paired), 'walker', scatter_dimens...  103 us
    all_to_all x1, blocking collectives, per_device(): lax.all_to_all(jnp.stack([col_shard] * lax.axis_size('prow')), 'prow', 0, 0)  65.9 us
    psum x1, blocking collectives, per_device(): lax.psum((column_sums(o_rows), column_sums(o_cols)), 'walker')  38.7 us
    all_gather x1, waiting for transfers between devices, per_device(): row_tile = lax.all_gather(row_shard, 'pcol', axis=1, tiled=True)  26.3 us
    dot_general x1, matrix products, tile_product(): lax.dot_general(row_tile, right_tile, (((0,), (0,)), ((), ())), preferred...  15.2 us
  transfers between devices with their start and end apart: 3, of which 2 were waited for; matrix products, arithmetic and copies ran while one was open for 4% of the time, Pallas kernels for 0%

profile of v1, /device:TPU:0, one launch (start us, length us, event | category | flops | bytes accessed | tf_op | source)
XLA Modules:
  0.0 277.8 jit_solution(1935094033432115249)
XLA Ops:
  7.2 0.0 copy-start.1
  7.2 0.0 copy-start
  7.2 0.0 all-gather.5.cloned.1.call-start
  7.2 0.7 all-gather.5.cloned.1.call-update
  7.9 0.0 all-gather.3.cloned.1.call-start
  8.0 1.5 convert_reduce_fusion.1
  9.5 0.0 copy-done
  9.5 0.3 convert_reduce_fusion
  9.8 38.7 %all-reduce = (f32[256]{0:T(256)S(1)}, f32[512]{0:T(512)S(1)}) all-reduce(f32[256]{0:T(256)S(1)} %convert_reduce_fusion.1, f32[512]{0:T(512)S(1)} %convert_reduce_fusion), channel_id=1, replica_groups=mesh['walker'=16,'prow'=2,'pcol'=4] {'walker'}, use_global_device_ids=true, to_apply=%region_1.0 | all-reduce | flops 768 | bytes 6144 | tf_op jit(solution)/shard_map/psum | solution.py:19
  48.5 0.0 copy-done.1
  48.5 1.2 fusion.5
  49.7 0.0 all-gather.3.cloned.1.call-update
  49.8 0.0 reduce-scatter.2.cloned.1.call-start
  49.8 0.4 fusion.6
  50.2 0.4 pad_maximum_fusion
  50.6 65.9 %all_to_all.5 = bf16[2,2048,512]{2,1,0:T(8,128)(2,1)S(1)} all-to-all(bf16[2,2048,512]{2,1,0:T(8,128)(2,1)S(1)} %pad_maximum_fusion), channel_id=1, replica_groups=mesh['walker'=16,'prow'=2,'pcol'=4] {'prow'}, dimensions={0} | all-to-all | bytes 8388608 | tf_op jit(solution)/shard_map/all_to_all | solution.py:25
  116.5 2.6 copy.7
  119.1 0.0 copy-done.2
  119.1 5.5 %add_convert_fusion = bf16[2048,1024]{1,0:T(8,128)(2,1)} fusion(bf16[2048,1024]{1,0:T(8,128)(2,1)} %all-gather.5.cloned.1.call-done, bf16[2048,1024]{1,0:T(8,128)(2,1)} %bitcast.7, f32[2048]{0:T(1024)S(1)} %copy-done.2), kind=kLoop, calls=%fused_computation.4 | loop fusion | flops 10485760 | bytes 12591104 | tf_op jit(solution)/shard_map/convert_element_type | solution.py:29
  124.6 26.3 %all-gather.3.cloned.1.call-done = bf16[2048,1024]{1,0:T(8,128)(2,1)} async-done(((bf16[2048,256]{1,0:T(8,128)(2,1)}), bf16[2048,1024]{1,0:T(8,128)(2,1)}) %all-gather.3.cloned.1.call-update) | async-done | bytes 4194320 | tf_op jit(solution)/shard_map/all_gather | solution.py:22
  150.9 15.2 %fusion = f32[1024,2048]{1,0:T(8,128)} fusion(bf16[2048,1024]{1,0:T(8,128)(2,1)} %all-gather.3.cloned.1.call-done, bf16[2048,1024]{1,0:T(8,128)(2,1)} %add_convert_fusion, bf16[2048,1024]{1,0:T(8,128)(2,1)} %bitcast.8), kind=kOutput, calls=%fused_computation | convolution fusion | flops 8606711808 | bytes 20971520 | tf_op jit(solution)/shard_map/dot_general | solution.py:12
  166.1 0.0 reduce-scatter.2.cloned.1.call-update
  166.1 103.3 %reduce-scatter.2.cloned.1.call-done = f32[64,2048]{1,0:T(8,128)} async-done(((f32[1024,2048]{1,0:T(8,128)}), f32[64,2048]{1,0:T(8,128)}) %reduce-scatter.2.cloned.1.call-update) | async-done | bytes 524304 | tf_op jit(solution)/shard_map/reduce_scatter | solution.py:31
  269.4 1.9 slice_multiply_fusion
  (4 shorter events, 0.0 us)
Async XLA Ops:
  7.2 41.4 %copy-start.1 = (bf16[2048,256]{1,0:T(8,128)(2,1)S(1)}, bf16[2048,256]{1,0:T(8,128)(2,1)}, u32[]{:S(2)}) copy-start(bf16[2048,256]{1,0:T(8,128)(2,1)} %param.4) | copy-start | bytes 3145732
  7.2 2.3 copy-start
  7.2 111.9 %all-gather.5.cloned.1.call-start = ((), (), s32[]{:S(2)}) async-start(), calls=%async_computation.3 | async-start | bytes 6291456 | tf_op jit(solution)/shard_map/all_gather | solution.py:27
  7.9 143.0 %all-gather.3.cloned.1.call-start = ((), (), s32[]{:S(2)}) async-start(), calls=%async_computation.2 | async-start | bytes 5242880 | tf_op jit(solution)/shard_map/all_gather | solution.py:22
  49.8 219.6 %reduce-scatter.2.cloned.1.call-start = ((), (), s32[]{:S(2)}) async-start(), calls=%async_computation.4 | async-start | bytes 8912896 | tf_op jit(solution)/shard_map/reduce_scatter | solution.py:31
  116.5 2.6 copy-start.2
Sparse Core Ops, SparseCore 0:
  9.6 80.8 all-gather.4
  92.1 58.7 all-gather.2
  166.2 103.1 reduce-scatter.1
